TPU v7x, 512 devices: a whole 4x4x16 slice. The times are simulated.
512 devices in a mesh: row: 8 (over y, z_hi), col: 16 (over z_lo, core), depth: 4 (over x).
Axes of the slice: x: 4, y: 4, z: 16 (z_hi: 2, z_lo: 8; z = z_hi * 8 + z_lo), core: 2. Of those that a mesh axis runs over, the one named last changes fastest.
Arguments:
- a_tiles: bfloat16 [8, 16, 4, 4, 128, 128], P('row', 'col', 'depth'), may hold values from -0.625 to 0.625
- pair_lists: int32 [8, 16, 4, 16, 2, 4, 12], P('row', 'col', 'depth'), may hold values from 0 to 31, as said below
Outputs:
- product_blocks: float32 [8, 16, 12, 128, 128], P('row', 'col', 'depth')
Inputs may be any that keep to these rules, and one draw needn't show every extreme that they name: pair_lists[..., 0, m, o] is a left slot below 4, or 4 for an empty pair slot; the live pairs of a product block come first; pair_lists[..., 1, m, o] is a slot of the right panel.
All inputs are finite; a program needn't handle non-finite values.
Results may differ from a plain program's by a relative error of at most 0.0003.
Values may be sent and summed in bfloat16 or wider, within the bound.
A program may use at most 64 MiB of HBM per device.

v0:
```python
import jax
import jax.numpy as jnp
from jax import lax
from jax.sharding import PartitionSpec as P


def from_behind(block, axis, distance):
    devices = range(lax.axis_size(axis))
    route = [((i - distance) % len(devices), i) for i in devices]
    return lax.ppermute(block, axis, route)


def body(a_tiles, pair_lists):
    slot_count = a_tiles.shape[3]
    block_width = a_tiles.shape[4]
    own_tiles = a_tiles.reshape(slot_count, block_width, block_width)
    pair_table = pair_lists.reshape(pair_lists.shape[3:])
    shift_count = pair_table.shape[0]
    right_panel = lax.all_gather(own_tiles, "row", axis=0, tiled=True)
    zero_block = jnp.zeros((1, block_width, block_width), jnp.bfloat16)

    def contract(left_set, left_index, right_index):
        chosen = jnp.take(left_set, left_index, axis=0)
        partner = jnp.take(right_panel, right_index, axis=0)
        return jnp.einsum("moik,mojk->oij", chosen, partner, preferred_element_type=jnp.float32)

    def advance(step_index, carried):
        panel_tile, running = carried
        shifted = from_behind(panel_tile, "col", 1)
        padded = jnp.concatenate([shifted, zero_block], axis=0)
        return (
            shifted,
            running + contract(padded, pair_table[step_index, 0], pair_table[step_index, 1]),
        )

    opening = contract(
        jnp.concatenate([own_tiles, zero_block], axis=0), pair_table[0, 0], pair_table[0, 1]
    )
    carried = lax.fori_loop(1, shift_count, advance, (own_tiles, opening))
    running = carried[1]
    reduced = lax.psum_scatter(running, "depth", scatter_dimension=0, tiled=True)
    return reduced.reshape((1, 1) + reduced.shape)


def solution(mesh):
    placed = (
        P("row", "col", "depth", None, None, None),
        P("row", "col", "depth", None, None, None, None),
    )
    return jax.shard_map(
        body,
        mesh=mesh,
        in_specs=placed,
        out_specs=P("row", "col", "depth", None, None),
        check_vma=False,
    )
```

profile of v0, /device:TPU:8, one launch (start us, length us, event | category | flops | bytes accessed | tf_op | source)
XLA Modules:
  0.0 410.4 jit_solution(16223850005393163813)
XLA Ops:
  11.3 94.5 %all-gather.3.cloned.1.call-done = bf16[1,1,1,32,128,128]{5,4,2,1,0,3:T(8,128)(2,1)} async-done(((bf16[1,1,1,4,128,128]{5,4,2,1,0,3:T(8,128)(2,1)}), bf16[1,1,1,32,128,128]{5,4,2,1,0,3:T(8,128)(2,1)}) %all-gather.3.cloned.1.call-update) | async-done | bytes 1048592 | tf_op jit(solution)/shard_map/all_gather | solution.py:19
  105.8 3.2 gather_fusion.3
  112.1 270.5 %while.17 = (s32[]{:T(128)}, bf16[4,128,128]{2,1,0:T(8,128)(2,1)S(1)}, f32[12,128,128]{2,1,0:T(8,128)}, s32[16,2,4,12]{3,2,1,0:T(4,128)S(1)}, bf16[32,128,128]{2...) while((s32[]{:T(128)}, bf16[4,128,128]{2,1,0:T(8,128)(2,1)S(1)}, ...), condition=%wide.region_1.0_spmd, body=%wide.region_0.3_spmd.sunk | while | flops 203098688 | bytes 12102445 | solution.py:39
  115.3 9.7 %collective-permute-done = bf16[4,128,128]{2,1,0:T(8,128)(2,1)S(1)} collective-permute-done((bf16[4,128,128]{2,1,0:T(8,128)(2,1)S(1)}, bf16[4,128,128]{2,1,0:T(8,128)(2,1)S(1)}, u32[]{:S(2)}, u32[]{:S(2)}) %collective-permute-start) | collective-permute-done | bytes 131104 | tf_op jit(solution)/shard_map/while/body/eval_jaxpr/ppermute | solution.py:10
  126.9 3.1 fusion.14
  133.3 9.7 %collective-permute-done = bf16[4,128,128]{2,1,0:T(8,128)(2,1)S(1)} collective-permute-done((bf16[4,128,128]{2,1,0:T(8,128)(2,1)S(1)}, bf16[4,128,128]{2,1,0:T(8,128)(2,1)S(1)}, u32[]{:S(2)}, u32[]{:S(2)}) %collective-permute-start) | collective-permute-done | bytes 131104 | tf_op jit(solution)/shard_map/while/body/eval_jaxpr/ppermute | solution.py:10
  145.0 3.1 fusion.14
  151.4 9.7 %collective-permute-done = bf16[4,128,128]{2,1,0:T(8,128)(2,1)S(1)} collective-permute-done((bf16[4,128,128]{2,1,0:T(8,128)(2,1)S(1)}, bf16[4,128,128]{2,1,0:T(8,128)(2,1)S(1)}, u32[]{:S(2)}, u32[]{:S(2)}) %collective-permute-start) | collective-permute-done | bytes 131104 | tf_op jit(solution)/shard_map/while/body/eval_jaxpr/ppermute | solution.py:10
  163.0 3.1 fusion.14
  169.4 9.7 %collective-permute-done = bf16[4,128,128]{2,1,0:T(8,128)(2,1)S(1)} collective-permute-done((bf16[4,128,128]{2,1,0:T(8,128)(2,1)S(1)}, bf16[4,128,128]{2,1,0:T(8,128)(2,1)S(1)}, u32[]{:S(2)}, u32[]{:S(2)}) %collective-permute-start) | collective-permute-done | bytes 131104 | tf_op jit(solution)/shard_map/while/body/eval_jaxpr/ppermute | solution.py:10
  187.4 9.7 %collective-permute-done = bf16[4,128,128]{2,1,0:T(8,128)(2,1)S(1)} collective-permute-done((bf16[4,128,128]{2,1,0:T(8,128)(2,1)S(1)}, bf16[4,128,128]{2,1,0:T(8,128)(2,1)S(1)}, u32[]{:S(2)}, u32[]{:S(2)}) %collective-permute-start) | collective-permute-done | bytes 131104 | tf_op jit(solution)/shard_map/while/body/eval_jaxpr/ppermute | solution.py:10
  199.1 3.1 fusion.14
  205.5 9.7 %collective-permute-done = bf16[4,128,128]{2,1,0:T(8,128)(2,1)S(1)} collective-permute-done((bf16[4,128,128]{2,1,0:T(8,128)(2,1)S(1)}, bf16[4,128,128]{2,1,0:T(8,128)(2,1)S(1)}, u32[]{:S(2)}, u32[]{:S(2)}) %collective-permute-start) | collective-permute-done | bytes 131104 | tf_op jit(solution)/shard_map/while/body/eval_jaxpr/ppermute | solution.py:10
  217.1 3.1 fusion.14
  223.5 9.7 %collective-permute-done = bf16[4,128,128]{2,1,0:T(8,128)(2,1)S(1)} collective-permute-done((bf16[4,128,128]{2,1,0:T(8,128)(2,1)S(1)}, bf16[4,128,128]{2,1,0:T(8,128)(2,1)S(1)}, u32[]{:S(2)}, u32[]{:S(2)}) %collective-permute-start) | collective-permute-done | bytes 131104 | tf_op jit(solution)/shard_map/while/body/eval_jaxpr/ppermute | solution.py:10
  241.5 9.7 %collective-permute-done = bf16[4,128,128]{2,1,0:T(8,128)(2,1)S(1)} collective-permute-done((bf16[4,128,128]{2,1,0:T(8,128)(2,1)S(1)}, bf16[4,128,128]{2,1,0:T(8,128)(2,1)S(1)}, u32[]{:S(2)}, u32[]{:S(2)}) %collective-permute-start) | collective-permute-done | bytes 131104 | tf_op jit(solution)/shard_map/while/body/eval_jaxpr/ppermute | solution.py:10
  259.6 9.7 %collective-permute-done = bf16[4,128,128]{2,1,0:T(8,128)(2,1)S(1)} collective-permute-done((bf16[4,128,128]{2,1,0:T(8,128)(2,1)S(1)}, bf16[4,128,128]{2,1,0:T(8,128)(2,1)S(1)}, u32[]{:S(2)}, u32[]{:S(2)}) %collective-permute-start) | collective-permute-done | bytes 131104 | tf_op jit(solution)/shard_map/while/body/eval_jaxpr/ppermute | solution.py:10
  277.6 9.7 %collective-permute-done = bf16[4,128,128]{2,1,0:T(8,128)(2,1)S(1)} collective-permute-done((bf16[4,128,128]{2,1,0:T(8,128)(2,1)S(1)}, bf16[4,128,128]{2,1,0:T(8,128)(2,1)S(1)}, u32[]{:S(2)}, u32[]{:S(2)}) %collective-permute-start) | collective-permute-done | bytes 131104 | tf_op jit(solution)/shard_map/while/body/eval_jaxpr/ppermute | solution.py:10
  295.6 9.7 %collective-permute-done = bf16[4,128,128]{2,1,0:T(8,128)(2,1)S(1)} collective-permute-done((bf16[4,128,128]{2,1,0:T(8,128)(2,1)S(1)}, bf16[4,128,128]{2,1,0:T(8,128)(2,1)S(1)}, u32[]{:S(2)}, u32[]{:S(2)}) %collective-permute-start) | collective-permute-done | bytes 131104 | tf_op jit(solution)/shard_map/while/body/eval_jaxpr/ppermute | solution.py:10
  313.7 9.7 %collective-permute-done = bf16[4,128,128]{2,1,0:T(8,128)(2,1)S(1)} collective-permute-done((bf16[4,128,128]{2,1,0:T(8,128)(2,1)S(1)}, bf16[4,128,128]{2,1,0:T(8,128)(2,1)S(1)}, u32[]{:S(2)}, u32[]{:S(2)}) %collective-permute-start) | collective-permute-done | bytes 131104 | tf_op jit(solution)/shard_map/while/body/eval_jaxpr/ppermute | solution.py:10
  331.7 9.7 %collective-permute-done = bf16[4,128,128]{2,1,0:T(8,128)(2,1)S(1)} collective-permute-done((bf16[4,128,128]{2,1,0:T(8,128)(2,1)S(1)}, bf16[4,128,128]{2,1,0:T(8,128)(2,1)S(1)}, u32[]{:S(2)}, u32[]{:S(2)}) %collective-permute-start) | collective-permute-done | bytes 131104 | tf_op jit(solution)/shard_map/while/body/eval_jaxpr/ppermute | solution.py:10
  349.8 9.7 %collective-permute-done = bf16[4,128,128]{2,1,0:T(8,128)(2,1)S(1)} collective-permute-done((bf16[4,128,128]{2,1,0:T(8,128)(2,1)S(1)}, bf16[4,128,128]{2,1,0:T(8,128)(2,1)S(1)}, u32[]{:S(2)}, u32[]{:S(2)}) %collective-permute-start) | collective-permute-done | bytes 131104 | tf_op jit(solution)/shard_map/while/body/eval_jaxpr/ppermute | solution.py:10
  367.8 9.7 %collective-permute-done = bf16[4,128,128]{2,1,0:T(8,128)(2,1)S(1)} collective-permute-done((bf16[4,128,128]{2,1,0:T(8,128)(2,1)S(1)}, bf16[4,128,128]{2,1,0:T(8,128)(2,1)S(1)}, u32[]{:S(2)}, u32[]{:S(2)}) %collective-permute-start) | collective-permute-done | bytes 131104 | tf_op jit(solution)/shard_map/while/body/eval_jaxpr/ppermute | solution.py:10
  382.6 21.0 %reduce-scatter.2.cloned.1.call-done = f32[3,128,128]{2,1,0:T(8,128)} async-done(((f32[12,128,128]{2,1,0:T(8,128)}), f32[3,128,128]{2,1,0:T(8,128)}) %reduce-scatter.2.cloned.1.call-update) | async-done | bytes 196624 | tf_op jit(solution)/shard_map/reduce_scatter | solution.py:41
  (211 shorter events, 116.7 us)
Async XLA Ops:
  6.5 99.3 %all-gather.3.cloned.1.call-start = ((), (), s32[]{:S(2)}) async-start(), calls=%async_computation.2 | async-start | bytes 1179648 | tf_op jit(solution)/shard_map/all_gather | solution.py:19
  8.1 395.5 %reduce-scatter.2.cloned.1.call-start = ((), (), s32[]{:S(2)}) async-start(), calls=%async_computation.1 | async-start | bytes 983040 | tf_op jit(solution)/shard_map/reduce_scatter | solution.py:41
  109.0 3.1 copy-start
  109.0 3.1 copy-start.1
  112.1 12.9 %collective-permute-start = (bf16[4,128,128]{2,1,0:T(8,128)(2,1)S(1)}, bf16[4,128,128]{2,1,0:T(8,128)(2,1)S(1)}, u32[]{:S(2)}, u32[]{:S(2)}) collective-permute-start(bf16[4,128,128]{2,1,0:T(8,128)(2,1)S(1)} %get-tuple-element.209), channel_id=1, source_target_pairs={{60,0},{0,4},{4,8},{8,12},{12,16},{16,20},{20,24},{24,28},{28,32},... | collective-permute-start | bytes 393224 | tf_op jit(solution)/shard_map/while/body/eval_jaxpr/ppermute | solution.py:10
  130.1 12.9 %collective-permute-start = (bf16[4,128,128]{2,1,0:T(8,128)(2,1)S(1)}, bf16[4,128,128]{2,1,0:T(8,128)(2,1)S(1)}, u32[]{:S(2)}, u32[]{:S(2)}) collective-permute-start(bf16[4,128,128]{2,1,0:T(8,128)(2,1)S(1)} %get-tuple-element.209), channel_id=1, source_target_pairs={{60,0},{0,4},{4,8},{8,12},{12,16},{16,20},{20,24},{24,28},{28,32},... | collective-permute-start | bytes 393224 | tf_op jit(solution)/shard_map/while/body/eval_jaxpr/ppermute | solution.py:10
  148.1 12.9 %collective-permute-start = (bf16[4,128,128]{2,1,0:T(8,128)(2,1)S(1)}, bf16[4,128,128]{2,1,0:T(8,128)(2,1)S(1)}, u32[]{:S(2)}, u32[]{:S(2)}) collective-permute-start(bf16[4,128,128]{2,1,0:T(8,128)(2,1)S(1)} %get-tuple-element.209), channel_id=1, source_target_pairs={{60,0},{0,4},{4,8},{8,12},{12,16},{16,20},{20,24},{24,28},{28,32},... | collective-permute-start | bytes 393224 | tf_op jit(solution)/shard_map/while/body/eval_jaxpr/ppermute | solution.py:10
  166.2 12.9 %collective-permute-start = (bf16[4,128,128]{2,1,0:T(8,128)(2,1)S(1)}, bf16[4,128,128]{2,1,0:T(8,128)(2,1)S(1)}, u32[]{:S(2)}, u32[]{:S(2)}) collective-permute-start(bf16[4,128,128]{2,1,0:T(8,128)(2,1)S(1)} %get-tuple-element.209), channel_id=1, source_target_pairs={{60,0},{0,4},{4,8},{8,12},{12,16},{16,20},{20,24},{24,28},{28,32},... | collective-permute-start | bytes 393224 | tf_op jit(solution)/shard_map/while/body/eval_jaxpr/ppermute | solution.py:10
  184.2 12.9 %collective-permute-start = (bf16[4,128,128]{2,1,0:T(8,128)(2,1)S(1)}, bf16[4,128,128]{2,1,0:T(8,128)(2,1)S(1)}, u32[]{:S(2)}, u32[]{:S(2)}) collective-permute-start(bf16[4,128,128]{2,1,0:T(8,128)(2,1)S(1)} %get-tuple-element.209), channel_id=1, source_target_pairs={{60,0},{0,4},{4,8},{8,12},{12,16},{16,20},{20,24},{24,28},{28,32},... | collective-permute-start | bytes 393224 | tf_op jit(solution)/shard_map/while/body/eval_jaxpr/ppermute | solution.py:10
  202.2 12.9 %collective-permute-start = (bf16[4,128,128]{2,1,0:T(8,128)(2,1)S(1)}, bf16[4,128,128]{2,1,0:T(8,128)(2,1)S(1)}, u32[]{:S(2)}, u32[]{:S(2)}) collective-permute-start(bf16[4,128,128]{2,1,0:T(8,128)(2,1)S(1)} %get-tuple-element.209), channel_id=1, source_target_pairs={{60,0},{0,4},{4,8},{8,12},{12,16},{16,20},{20,24},{24,28},{28,32},... | collective-permute-start | bytes 393224 | tf_op jit(solution)/shard_map/while/body/eval_jaxpr/ppermute | solution.py:10
  220.3 12.9 %collective-permute-start = (bf16[4,128,128]{2,1,0:T(8,128)(2,1)S(1)}, bf16[4,128,128]{2,1,0:T(8,128)(2,1)S(1)}, u32[]{:S(2)}, u32[]{:S(2)}) collective-permute-start(bf16[4,128,128]{2,1,0:T(8,128)(2,1)S(1)} %get-tuple-element.209), channel_id=1, source_target_pairs={{60,0},{0,4},{4,8},{8,12},{12,16},{16,20},{20,24},{24,28},{28,32},... | collective-permute-start | bytes 393224 | tf_op jit(solution)/shard_map/while/body/eval_jaxpr/ppermute | solution.py:10
  238.3 12.9 %collective-permute-start = (bf16[4,128,128]{2,1,0:T(8,128)(2,1)S(1)}, bf16[4,128,128]{2,1,0:T(8,128)(2,1)S(1)}, u32[]{:S(2)}, u32[]{:S(2)}) collective-permute-start(bf16[4,128,128]{2,1,0:T(8,128)(2,1)S(1)} %get-tuple-element.209), channel_id=1, source_target_pairs={{60,0},{0,4},{4,8},{8,12},{12,16},{16,20},{20,24},{24,28},{28,32},... | collective-permute-start | bytes 393224 | tf_op jit(solution)/shard_map/while/body/eval_jaxpr/ppermute | solution.py:10
  256.3 12.9 %collective-permute-start = (bf16[4,128,128]{2,1,0:T(8,128)(2,1)S(1)}, bf16[4,128,128]{2,1,0:T(8,128)(2,1)S(1)}, u32[]{:S(2)}, u32[]{:S(2)}) collective-permute-start(bf16[4,128,128]{2,1,0:T(8,128)(2,1)S(1)} %get-tuple-element.209), channel_id=1, source_target_pairs={{60,0},{0,4},{4,8},{8,12},{12,16},{16,20},{20,24},{24,28},{28,32},... | collective-permute-start | bytes 393224 | tf_op jit(solution)/shard_map/while/body/eval_jaxpr/ppermute | solution.py:10
  274.4 12.9 %collective-permute-start = (bf16[4,128,128]{2,1,0:T(8,128)(2,1)S(1)}, bf16[4,128,128]{2,1,0:T(8,128)(2,1)S(1)}, u32[]{:S(2)}, u32[]{:S(2)}) collective-permute-start(bf16[4,128,128]{2,1,0:T(8,128)(2,1)S(1)} %get-tuple-element.209), channel_id=1, source_target_pairs={{60,0},{0,4},{4,8},{8,12},{12,16},{16,20},{20,24},{24,28},{28,32},... | collective-permute-start | bytes 393224 | tf_op jit(solution)/shard_map/while/body/eval_jaxpr/ppermute | solution.py:10
  292.4 12.9 %collective-permute-start = (bf16[4,128,128]{2,1,0:T(8,128)(2,1)S(1)}, bf16[4,128,128]{2,1,0:T(8,128)(2,1)S(1)}, u32[]{:S(2)}, u32[]{:S(2)}) collective-permute-start(bf16[4,128,128]{2,1,0:T(8,128)(2,1)S(1)} %get-tuple-element.209), channel_id=1, source_target_pairs={{60,0},{0,4},{4,8},{8,12},{12,16},{16,20},{20,24},{24,28},{28,32},... | collective-permute-start | bytes 393224 | tf_op jit(solution)/shard_map/while/body/eval_jaxpr/ppermute | solution.py:10
  310.5 12.9 %collective-permute-start = (bf16[4,128,128]{2,1,0:T(8,128)(2,1)S(1)}, bf16[4,128,128]{2,1,0:T(8,128)(2,1)S(1)}, u32[]{:S(2)}, u32[]{:S(2)}) collective-permute-start(bf16[4,128,128]{2,1,0:T(8,128)(2,1)S(1)} %get-tuple-element.209), channel_id=1, source_target_pairs={{60,0},{0,4},{4,8},{8,12},{12,16},{16,20},{20,24},{24,28},{28,32},... | collective-permute-start | bytes 393224 | tf_op jit(solution)/shard_map/while/body/eval_jaxpr/ppermute | solution.py:10
  328.5 12.9 %collective-permute-start = (bf16[4,128,128]{2,1,0:T(8,128)(2,1)S(1)}, bf16[4,128,128]{2,1,0:T(8,128)(2,1)S(1)}, u32[]{:S(2)}, u32[]{:S(2)}) collective-permute-start(bf16[4,128,128]{2,1,0:T(8,128)(2,1)S(1)} %get-tuple-element.209), channel_id=1, source_target_pairs={{60,0},{0,4},{4,8},{8,12},{12,16},{16,20},{20,24},{24,28},{28,32},... | collective-permute-start | bytes 393224 | tf_op jit(solution)/shard_map/while/body/eval_jaxpr/ppermute | solution.py:10
  346.5 12.9 %collective-permute-start = (bf16[4,128,128]{2,1,0:T(8,128)(2,1)S(1)}, bf16[4,128,128]{2,1,0:T(8,128)(2,1)S(1)}, u32[]{:S(2)}, u32[]{:S(2)}) collective-permute-start(bf16[4,128,128]{2,1,0:T(8,128)(2,1)S(1)} %get-tuple-element.209), channel_id=1, source_target_pairs={{60,0},{0,4},{4,8},{8,12},{12,16},{16,20},{20,24},{24,28},{28,32},... | collective-permute-start | bytes 393224 | tf_op jit(solution)/shard_map/while/body/eval_jaxpr/ppermute | solution.py:10
  364.6 12.9 %collective-permute-start = (bf16[4,128,128]{2,1,0:T(8,128)(2,1)S(1)}, bf16[4,128,128]{2,1,0:T(8,128)(2,1)S(1)}, u32[]{:S(2)}, u32[]{:S(2)}) collective-permute-start(bf16[4,128,128]{2,1,0:T(8,128)(2,1)S(1)} %get-tuple-element.209), channel_id=1, source_target_pairs={{60,0},{0,4},{4,8},{8,12},{12,16},{16,20},{20,24},{24,28},{28,32},... | collective-permute-start | bytes 393224 | tf_op jit(solution)/shard_map/while/body/eval_jaxpr/ppermute | solution.py:10
Sparse Core Ops, SparseCore 0:
  10.6 95.2 all-gather.2
  382.7 20.7 reduce-scatter.1
where the time goes:
time: 412 us; the launch traced here: 410 us
  waiting for transfers between devices  261 us (63%)
  local copies, waits for them, and re-layouts  56 us (14%)
  matrix products  50.3 us (12%)
  starting transfers between devices  28.8 us (7%)
  between operations  13.4 us (3%)
    ppermute x15, waiting for transfers between devices, from_behind(): return lax.ppermute(block, axis, route)  145 us
    all_gather x1, waiting for transfers between devices, body(): right_panel = lax.all_gather(own_tiles, 'row', axis=0, tiled=True)  94.5 us
    dot_general x16, matrix products, contract(): jnp.einsum('moik,mojk->oij', chosen, partner, preferred_element_type=jnp....  50.3 us
    gather x16, local copies, waits for them, and re-layouts, contract(): chosen = jnp.take(left_set, left_index, axis=0)  30.1 us
    ppermute x15, starting transfers between devices, from_behind(): return lax.ppermute(block, axis, route)  28.8 us
    reduce_scatter x1, waiting for transfers between devices, body(): lax.psum_scatter(running, 'depth', scatter_dimension=0, tiled=True)  21 us
    gather x16, local copies, waits for them, and re-layouts, contract(): partner = jnp.take(right_panel, right_index, axis=0)  15.9 us
  transfers between devices with their start and end apart: 17, of which 17 were waited for; matrix products, arithmetic and copies ran while one was open for 5% of the time, Pallas kernels for 0%

commit v1 on v0

--- a/solution.py
+++ b/solution.py
@@ -16,7 +16,9 @@
     own_tiles = a_tiles.reshape(slot_count, block_width, block_width)
     pair_table = pair_lists.reshape(pair_lists.shape[3:])
     shift_count = pair_table.shape[0]
-    right_panel = lax.all_gather(own_tiles, "row", axis=0, tiled=True)
+    right_panel = jnp.concatenate(
+        lax.all_to_all(jnp.stack([own_tiles] * lax.axis_size("row")), "row", 0, 0), axis=0
+    )
     zero_block = jnp.zeros((1, block_width, block_width), jnp.bfloat16)
 
     def contract(left_set, left_index, right_index):

time: 412 us -> 371 us (0.900)
  waiting for transfers between devices: 261 us -> 195 us
  starting transfers between devices: 28.8 us -> 56.7 us
    all_gather x1 -> x0, waiting for transfers between devices: 94.5 us -> none  [body(): right_panel = lax.all_gather(own_tiles, 'row', axis=0, tiled=True)]
    all_to_all x0 -> x1, waiting for transfers between devices: none -> 25.2 us  [body(): lax.all_to_all(jnp.stack([own_tiles] * lax.axis_size('row')), 'row', 0, 0)]
    all_to_all x0 -> x1, starting transfers between devices: none -> 18.2 us  [body(): lax.all_to_all(jnp.stack([own_tiles] * lax.axis_size('row')), 'row', 0, 0)]
    ppermute x15, starting transfers between devices: 28.8 us -> 38.5 us  [from_behind(): return lax.ppermute(block, axis, route)]
  transfers between devices with their start and end apart: 17 -> 17, of which waited for: 17 -> 17; matrix products, arithmetic and copies ran while one was open for 5% -> 6% of each run, Pallas kernels for 0% -> 0%
where the time goes in v1:
time: 371 us; the launch traced here: 370 us
  waiting for transfers between devices  195 us (53%)
  starting transfers between devices  56.7 us (15%)
  local copies, waits for them, and re-layouts  53.6 us (14%)
  matrix products  50.1 us (14%)
  between operations  13.4 us (4%)
    ppermute x15, waiting for transfers between devices, from_behind(): return lax.ppermute(block, axis, route)  148 us
    dot_general x16, matrix products, contract(): jnp.einsum('moik,mojk->oij', chosen, partner, preferred_element_type=jnp....  50.1 us
    ppermute x15, starting transfers between devices, from_behind(): return lax.ppermute(block, axis, route)  38.5 us
    gather x16, local copies, waits for them, and re-layouts, contract(): chosen = jnp.take(left_set, left_index, axis=0)  30.1 us
    all_to_all x1, waiting for transfers between devices, body(): lax.all_to_all(jnp.stack([own_tiles] * lax.axis_size('row')), 'row', 0, 0)  25.2 us
    reduce_scatter x1, waiting for transfers between devices, body(): lax.psum_scatter(running, 'depth', scatter_dimension=0, tiled=True)  21.4 us
    all_to_all x1, starting transfers between devices, body(): lax.all_to_all(jnp.stack([own_tiles] * lax.axis_size('row')), 'row', 0, 0)  18.2 us
    gather x16, local copies, waits for them, and re-layouts, contract(): partner = jnp.take(right_panel, right_index, axis=0)  14.7 us
  transfers between devices with their start and end apart: 17, of which 17 were waited for; matrix products, arithmetic and copies ran while one was open for 6% of the time, Pallas kernels for 0%

profile of v1, /device:TPU:8, one launch (start us, length us, event | category | flops | bytes accessed | tf_op | source)
XLA Modules:
  0.0 369.9 jit_solution(18383140428410427107)
XLA Ops:
  8.6 18.2 %all-to-all-start = ((bf16[8,4,128,128]{3,2,1,0:T(8,128)(2,1)}), bf16[8,4,128,128]{3,2,1,0:T(8,128)(2,1)S(1)}, u32[]{:S(2)}, u32[]{:S(2)}) async-start(bf16[8,4,128,128]{3,2,1,0:T(8,128)(2,1)} %stack.3), calls=%async_computation | async-start | bytes 2097152 | tf_op jit(solution)/shard_map/all_to_all | solution.py:20
  28.3 25.2 %all-to-all-done = bf16[8,4,128,128]{3,2,1,0:T(8,128)(2,1)S(1)} async-done(((bf16[8,4,128,128]{3,2,1,0:T(8,128)(2,1)}), bf16[8,4,128,128]{3,2,1,0:T(8,128)(2,1)S(1)}, u32[]{:S(2)}, u32[]{:S(2)}) %all-to-all-start) | async-done | bytes 1048608 | tf_op jit(solution)/shard_map/all_to_all | solution.py:20
  58.3 283.3 %while.17 = (s32[]{:T(128)}, bf16[4,128,128]{2,1,0:T(8,128)(2,1)S(1)}, f32[12,128,128]{2,1,0:T(8,128)}, s32[16,2,4,12]{3,2,1,0:T(4,128)S(1)}, bf16[32,128,128]{2...) while((s32[]{:T(128)}, bf16[4,128,128]{2,1,0:T(8,128)(2,1)S(1)}, ...), condition=%wide.region_1.0_spmd, body=%wide.region_0.3_spmd.sunk | while | flops 203098688 | bytes 12102445 | solution.py:41
  61.6 22.6 %collective-permute-done = bf16[4,128,128]{2,1,0:T(8,128)(2,1)S(1)} collective-permute-done((bf16[4,128,128]{2,1,0:T(8,128)(2,1)S(1)}, bf16[4,128,128]{2,1,0:T(8,128)(2,1)S(1)}, u32[]{:S(2)}, u32[]{:S(2)}) %collective-permute-start) | collective-permute-done | bytes 131104 | tf_op jit(solution)/shard_map/while/body/eval_jaxpr/ppermute | solution.py:10
  86.1 3.1 fusion.14
  89.3 10.1 %collective-permute-start = (bf16[4,128,128]{2,1,0:T(8,128)(2,1)S(1)}, bf16[4,128,128]{2,1,0:T(8,128)(2,1)S(1)}, u32[]{:S(2)}, u32[]{:S(2)}) collective-permute-start(bf16[4,128,128]{2,1,0:T(8,128)(2,1)S(1)} %get-tuple-element.209), channel_id=1, source_target_pairs={{60,0},{0,4},{4,8},{8,12},{12,16},{16,20},{20,24},{24,28},{28,32},... | collective-permute-start | bytes 393224 | tf_op jit(solution)/shard_map/while/body/eval_jaxpr/ppermute | solution.py:10
  107.3 3.5 collective-permute-start
  112.1 8.1 %collective-permute-done = bf16[4,128,128]{2,1,0:T(8,128)(2,1)S(1)} collective-permute-done((bf16[4,128,128]{2,1,0:T(8,128)(2,1)S(1)}, bf16[4,128,128]{2,1,0:T(8,128)(2,1)S(1)}, u32[]{:S(2)}, u32[]{:S(2)}) %collective-permute-start) | collective-permute-done | bytes 131104 | tf_op jit(solution)/shard_map/while/body/eval_jaxpr/ppermute | solution.py:10
  122.2 3.1 fusion.14
  128.6 9.7 %collective-permute-done = bf16[4,128,128]{2,1,0:T(8,128)(2,1)S(1)} collective-permute-done((bf16[4,128,128]{2,1,0:T(8,128)(2,1)S(1)}, bf16[4,128,128]{2,1,0:T(8,128)(2,1)S(1)}, u32[]{:S(2)}, u32[]{:S(2)}) %collective-permute-start) | collective-permute-done | bytes 131104 | tf_op jit(solution)/shard_map/while/body/eval_jaxpr/ppermute | solution.py:10
  140.2 3.1 fusion.14
  146.6 9.7 %collective-permute-done = bf16[4,128,128]{2,1,0:T(8,128)(2,1)S(1)} collective-permute-done((bf16[4,128,128]{2,1,0:T(8,128)(2,1)S(1)}, bf16[4,128,128]{2,1,0:T(8,128)(2,1)S(1)}, u32[]{:S(2)}, u32[]{:S(2)}) %collective-permute-start) | collective-permute-done | bytes 131104 | tf_op jit(solution)/shard_map/while/body/eval_jaxpr/ppermute | solution.py:10
  164.6 9.7 %collective-permute-done = bf16[4,128,128]{2,1,0:T(8,128)(2,1)S(1)} collective-permute-done((bf16[4,128,128]{2,1,0:T(8,128)(2,1)S(1)}, bf16[4,128,128]{2,1,0:T(8,128)(2,1)S(1)}, u32[]{:S(2)}, u32[]{:S(2)}) %collective-permute-start) | collective-permute-done | bytes 131104 | tf_op jit(solution)/shard_map/while/body/eval_jaxpr/ppermute | solution.py:10
  182.6 9.7 %collective-permute-done = bf16[4,128,128]{2,1,0:T(8,128)(2,1)S(1)} collective-permute-done((bf16[4,128,128]{2,1,0:T(8,128)(2,1)S(1)}, bf16[4,128,128]{2,1,0:T(8,128)(2,1)S(1)}, u32[]{:S(2)}, u32[]{:S(2)}) %collective-permute-start) | collective-permute-done | bytes 131104 | tf_op jit(solution)/shard_map/while/body/eval_jaxpr/ppermute | solution.py:10
  194.3 3.1 fusion.14
  200.7 9.7 %collective-permute-done = bf16[4,128,128]{2,1,0:T(8,128)(2,1)S(1)} collective-permute-done((bf16[4,128,128]{2,1,0:T(8,128)(2,1)S(1)}, bf16[4,128,128]{2,1,0:T(8,128)(2,1)S(1)}, u32[]{:S(2)}, u32[]{:S(2)}) %collective-permute-start) | collective-permute-done | bytes 131104 | tf_op jit(solution)/shard_map/while/body/eval_jaxpr/ppermute | solution.py:10
  218.7 9.7 %collective-permute-done = bf16[4,128,128]{2,1,0:T(8,128)(2,1)S(1)} collective-permute-done((bf16[4,128,128]{2,1,0:T(8,128)(2,1)S(1)}, bf16[4,128,128]{2,1,0:T(8,128)(2,1)S(1)}, u32[]{:S(2)}, u32[]{:S(2)}) %collective-permute-start) | collective-permute-done | bytes 131104 | tf_op jit(solution)/shard_map/while/body/eval_jaxpr/ppermute | solution.py:10
  236.7 9.7 %collective-permute-done = bf16[4,128,128]{2,1,0:T(8,128)(2,1)S(1)} collective-permute-done((bf16[4,128,128]{2,1,0:T(8,128)(2,1)S(1)}, bf16[4,128,128]{2,1,0:T(8,128)(2,1)S(1)}, u32[]{:S(2)}, u32[]{:S(2)}) %collective-permute-start) | collective-permute-done | bytes 131104 | tf_op jit(solution)/shard_map/while/body/eval_jaxpr/ppermute | solution.py:10
  254.7 9.7 %collective-permute-done = bf16[4,128,128]{2,1,0:T(8,128)(2,1)S(1)} collective-permute-done((bf16[4,128,128]{2,1,0:T(8,128)(2,1)S(1)}, bf16[4,128,128]{2,1,0:T(8,128)(2,1)S(1)}, u32[]{:S(2)}, u32[]{:S(2)}) %collective-permute-start) | collective-permute-done | bytes 131104 | tf_op jit(solution)/shard_map/while/body/eval_jaxpr/ppermute | solution.py:10
  272.8 9.7 %collective-permute-done = bf16[4,128,128]{2,1,0:T(8,128)(2,1)S(1)} collective-permute-done((bf16[4,128,128]{2,1,0:T(8,128)(2,1)S(1)}, bf16[4,128,128]{2,1,0:T(8,128)(2,1)S(1)}, u32[]{:S(2)}, u32[]{:S(2)}) %collective-permute-start) | collective-permute-done | bytes 131104 | tf_op jit(solution)/shard_map/while/body/eval_jaxpr/ppermute | solution.py:10
  290.8 9.7 %collective-permute-done = bf16[4,128,128]{2,1,0:T(8,128)(2,1)S(1)} collective-permute-done((bf16[4,128,128]{2,1,0:T(8,128)(2,1)S(1)}, bf16[4,128,128]{2,1,0:T(8,128)(2,1)S(1)}, u32[]{:S(2)}, u32[]{:S(2)}) %collective-permute-start) | collective-permute-done | bytes 131104 | tf_op jit(solution)/shard_map/while/body/eval_jaxpr/ppermute | solution.py:10
  308.8 9.7 %collective-permute-done = bf16[4,128,128]{2,1,0:T(8,128)(2,1)S(1)} collective-permute-done((bf16[4,128,128]{2,1,0:T(8,128)(2,1)S(1)}, bf16[4,128,128]{2,1,0:T(8,128)(2,1)S(1)}, u32[]{:S(2)}, u32[]{:S(2)}) %collective-permute-start) | collective-permute-done | bytes 131104 | tf_op jit(solution)/shard_map/while/body/eval_jaxpr/ppermute | solution.py:10
  326.8 9.7 %collective-permute-done = bf16[4,128,128]{2,1,0:T(8,128)(2,1)S(1)} collective-permute-done((bf16[4,128,128]{2,1,0:T(8,128)(2,1)S(1)}, bf16[4,128,128]{2,1,0:T(8,128)(2,1)S(1)}, u32[]{:S(2)}, u32[]{:S(2)}) %collective-permute-start) | collective-permute-done | bytes 131104 | tf_op jit(solution)/shard_map/while/body/eval_jaxpr/ppermute | solution.py:10
  341.7 21.4 %reduce-scatter.2.cloned.1.call-done = f32[3,128,128]{2,1,0:T(8,128)} async-done(((f32[12,128,128]{2,1,0:T(8,128)}), f32[3,128,128]{2,1,0:T(8,128)}) %reduce-scatter.2.cloned.1.call-update) | async-done | bytes 196624 | tf_op jit(solution)/shard_map/reduce_scatter | solution.py:43
  (209 shorter events, 118.0 us)
Async XLA Ops:
  7.4 19.4 %copy-start = (s32[1,1,1,16,2,4,12]{3,5,6,4,2,1,0:T(4,128)S(1)}, s32[1,1,1,16,2,4,12]{3,5,6,4,2,1,0:T(4,128)}, u32[]{:S(2)}) copy-start(s32[1,1,1,16,2,4,12]{3,5,6,4,2,1,0:T(4,128)} %param.9) | copy-start | bytes 18436
  8.6 44.8 %all-to-all-start = ((bf16[8,4,128,128]{3,2,1,0:T(8,128)(2,1)}), bf16[8,4,128,128]{3,2,1,0:T(8,128)(2,1)S(1)}, u32[]{:S(2)}, u32[]{:S(2)}) async-start(bf16[8,4,128,128]{3,2,1,0:T(8,128)(2,1)} %stack.3), calls=%async_computation | async-start | bytes 2097152 | tf_op jit(solution)/shard_map/all_to_all | solution.py:20
  26.8 336.2 %reduce-scatter.2.cloned.1.call-start = ((), (), s32[]{:S(2)}) async-start(), calls=%async_computation.2 | async-start | bytes 983040 | tf_op jit(solution)/shard_map/reduce_scatter | solution.py:43
  58.3 25.8 %collective-permute-start = (bf16[4,128,128]{2,1,0:T(8,128)(2,1)S(1)}, bf16[4,128,128]{2,1,0:T(8,128)(2,1)S(1)}, u32[]{:S(2)}, u32[]{:S(2)}) collective-permute-start(bf16[4,128,128]{2,1,0:T(8,128)(2,1)S(1)} %get-tuple-element.209), channel_id=1, source_target_pairs={{60,0},{0,4},{4,8},{8,12},{12,16},{16,20},{20,24},{24,28},{28,32},... | collective-permute-start | bytes 393224 | tf_op jit(solution)/shard_map/while/body/eval_jaxpr/ppermute | solution.py:10
  89.3 12.9 %collective-permute-start = (bf16[4,128,128]{2,1,0:T(8,128)(2,1)S(1)}, bf16[4,128,128]{2,1,0:T(8,128)(2,1)S(1)}, u32[]{:S(2)}, u32[]{:S(2)}) collective-permute-start(bf16[4,128,128]{2,1,0:T(8,128)(2,1)S(1)} %get-tuple-element.209), channel_id=1, source_target_pairs={{60,0},{0,4},{4,8},{8,12},{12,16},{16,20},{20,24},{24,28},{28,32},... | collective-permute-start | bytes 393224 | tf_op jit(solution)/shard_map/while/body/eval_jaxpr/ppermute | solution.py:10
  107.3 12.9 %collective-permute-start = (bf16[4,128,128]{2,1,0:T(8,128)(2,1)S(1)}, bf16[4,128,128]{2,1,0:T(8,128)(2,1)S(1)}, u32[]{:S(2)}, u32[]{:S(2)}) collective-permute-start(bf16[4,128,128]{2,1,0:T(8,128)(2,1)S(1)} %get-tuple-element.209), channel_id=1, source_target_pairs={{60,0},{0,4},{4,8},{8,12},{12,16},{16,20},{20,24},{24,28},{28,32},... | collective-permute-start | bytes 393224 | tf_op jit(solution)/shard_map/while/body/eval_jaxpr/ppermute | solution.py:10
  125.3 12.9 %collective-permute-start = (bf16[4,128,128]{2,1,0:T(8,128)(2,1)S(1)}, bf16[4,128,128]{2,1,0:T(8,128)(2,1)S(1)}, u32[]{:S(2)}, u32[]{:S(2)}) collective-permute-start(bf16[4,128,128]{2,1,0:T(8,128)(2,1)S(1)} %get-tuple-element.209), channel_id=1, source_target_pairs={{60,0},{0,4},{4,8},{8,12},{12,16},{16,20},{20,24},{24,28},{28,32},... | collective-permute-start | bytes 393224 | tf_op jit(solution)/shard_map/while/body/eval_jaxpr/ppermute | solution.py:10
  143.4 12.9 %collective-permute-start = (bf16[4,128,128]{2,1,0:T(8,128)(2,1)S(1)}, bf16[4,128,128]{2,1,0:T(8,128)(2,1)S(1)}, u32[]{:S(2)}, u32[]{:S(2)}) collective-permute-start(bf16[4,128,128]{2,1,0:T(8,128)(2,1)S(1)} %get-tuple-element.209), channel_id=1, source_target_pairs={{60,0},{0,4},{4,8},{8,12},{12,16},{16,20},{20,24},{24,28},{28,32},... | collective-permute-start | bytes 393224 | tf_op jit(solution)/shard_map/while/body/eval_jaxpr/ppermute | solution.py:10
  161.4 12.9 %collective-permute-start = (bf16[4,128,128]{2,1,0:T(8,128)(2,1)S(1)}, bf16[4,128,128]{2,1,0:T(8,128)(2,1)S(1)}, u32[]{:S(2)}, u32[]{:S(2)}) collective-permute-start(bf16[4,128,128]{2,1,0:T(8,128)(2,1)S(1)} %get-tuple-element.209), channel_id=1, source_target_pairs={{60,0},{0,4},{4,8},{8,12},{12,16},{16,20},{20,24},{24,28},{28,32},... | collective-permute-start | bytes 393224 | tf_op jit(solution)/shard_map/while/body/eval_jaxpr/ppermute | solution.py:10
  179.4 12.9 %collective-permute-start = (bf16[4,128,128]{2,1,0:T(8,128)(2,1)S(1)}, bf16[4,128,128]{2,1,0:T(8,128)(2,1)S(1)}, u32[]{:S(2)}, u32[]{:S(2)}) collective-permute-start(bf16[4,128,128]{2,1,0:T(8,128)(2,1)S(1)} %get-tuple-element.209), channel_id=1, source_target_pairs={{60,0},{0,4},{4,8},{8,12},{12,16},{16,20},{20,24},{24,28},{28,32},... | collective-permute-start | bytes 393224 | tf_op jit(solution)/shard_map/while/body/eval_jaxpr/ppermute | solution.py:10
  197.4 12.9 %collective-permute-start = (bf16[4,128,128]{2,1,0:T(8,128)(2,1)S(1)}, bf16[4,128,128]{2,1,0:T(8,128)(2,1)S(1)}, u32[]{:S(2)}, u32[]{:S(2)}) collective-permute-start(bf16[4,128,128]{2,1,0:T(8,128)(2,1)S(1)} %get-tuple-element.209), channel_id=1, source_target_pairs={{60,0},{0,4},{4,8},{8,12},{12,16},{16,20},{20,24},{24,28},{28,32},... | collective-permute-start | bytes 393224 | tf_op jit(solution)/shard_map/while/body/eval_jaxpr/ppermute | solution.py:10
  215.5 12.9 %collective-permute-start = (bf16[4,128,128]{2,1,0:T(8,128)(2,1)S(1)}, bf16[4,128,128]{2,1,0:T(8,128)(2,1)S(1)}, u32[]{:S(2)}, u32[]{:S(2)}) collective-permute-start(bf16[4,128,128]{2,1,0:T(8,128)(2,1)S(1)} %get-tuple-element.209), channel_id=1, source_target_pairs={{60,0},{0,4},{4,8},{8,12},{12,16},{16,20},{20,24},{24,28},{28,32},... | collective-permute-start | bytes 393224 | tf_op jit(solution)/shard_map/while/body/eval_jaxpr/ppermute | solution.py:10
  233.5 12.9 %collective-permute-start = (bf16[4,128,128]{2,1,0:T(8,128)(2,1)S(1)}, bf16[4,128,128]{2,1,0:T(8,128)(2,1)S(1)}, u32[]{:S(2)}, u32[]{:S(2)}) collective-permute-start(bf16[4,128,128]{2,1,0:T(8,128)(2,1)S(1)} %get-tuple-element.209), channel_id=1, source_target_pairs={{60,0},{0,4},{4,8},{8,12},{12,16},{16,20},{20,24},{24,28},{28,32},... | collective-permute-start | bytes 393224 | tf_op jit(solution)/shard_map/while/body/eval_jaxpr/ppermute | solution.py:10
  251.5 12.9 %collective-permute-start = (bf16[4,128,128]{2,1,0:T(8,128)(2,1)S(1)}, bf16[4,128,128]{2,1,0:T(8,128)(2,1)S(1)}, u32[]{:S(2)}, u32[]{:S(2)}) collective-permute-start(bf16[4,128,128]{2,1,0:T(8,128)(2,1)S(1)} %get-tuple-element.209), channel_id=1, source_target_pairs={{60,0},{0,4},{4,8},{8,12},{12,16},{16,20},{20,24},{24,28},{28,32},... | collective-permute-start | bytes 393224 | tf_op jit(solution)/shard_map/while/body/eval_jaxpr/ppermute | solution.py:10
  269.5 12.9 %collective-permute-start = (bf16[4,128,128]{2,1,0:T(8,128)(2,1)S(1)}, bf16[4,128,128]{2,1,0:T(8,128)(2,1)S(1)}, u32[]{:S(2)}, u32[]{:S(2)}) collective-permute-start(bf16[4,128,128]{2,1,0:T(8,128)(2,1)S(1)} %get-tuple-element.209), channel_id=1, source_target_pairs={{60,0},{0,4},{4,8},{8,12},{12,16},{16,20},{20,24},{24,28},{28,32},... | collective-permute-start | bytes 393224 | tf_op jit(solution)/shard_map/while/body/eval_jaxpr/ppermute | solution.py:10
  287.6 12.9 %collective-permute-start = (bf16[4,128,128]{2,1,0:T(8,128)(2,1)S(1)}, bf16[4,128,128]{2,1,0:T(8,128)(2,1)S(1)}, u32[]{:S(2)}, u32[]{:S(2)}) collective-permute-start(bf16[4,128,128]{2,1,0:T(8,128)(2,1)S(1)} %get-tuple-element.209), channel_id=1, source_target_pairs={{60,0},{0,4},{4,8},{8,12},{12,16},{16,20},{20,24},{24,28},{28,32},... | collective-permute-start | bytes 393224 | tf_op jit(solution)/shard_map/while/body/eval_jaxpr/ppermute | solution.py:10
  305.6 12.9 %collective-permute-start = (bf16[4,128,128]{2,1,0:T(8,128)(2,1)S(1)}, bf16[4,128,128]{2,1,0:T(8,128)(2,1)S(1)}, u32[]{:S(2)}, u32[]{:S(2)}) collective-permute-start(bf16[4,128,128]{2,1,0:T(8,128)(2,1)S(1)} %get-tuple-element.209), channel_id=1, source_target_pairs={{60,0},{0,4},{4,8},{8,12},{12,16},{16,20},{20,24},{24,28},{28,32},... | collective-permute-start | bytes 393224 | tf_op jit(solution)/shard_map/while/body/eval_jaxpr/ppermute | solution.py:10
  323.6 12.9 %collective-permute-start = (bf16[4,128,128]{2,1,0:T(8,128)(2,1)S(1)}, bf16[4,128,128]{2,1,0:T(8,128)(2,1)S(1)}, u32[]{:S(2)}, u32[]{:S(2)}) collective-permute-start(bf16[4,128,128]{2,1,0:T(8,128)(2,1)S(1)} %get-tuple-element.209), channel_id=1, source_target_pairs={{60,0},{0,4},{4,8},{8,12},{12,16},{16,20},{20,24},{24,28},{28,32},... | collective-permute-start | bytes 393224 | tf_op jit(solution)/shard_map/while/body/eval_jaxpr/ppermute | solution.py:10
Sparse Core Ops, SparseCore 0:
  341.8 21.2 reduce-scatter.1
